TPU v7x, 256 devices: a whole 4x4x8 slice. The times are simulated.
256 devices in a mesh: dp: 32 (over y, z), vocab: 8 (over x, core).
Axes of the slice: x: 4, y: 4, z: 8, core: 2. Of those that a mesh axis runs over, the one named last changes fastest.
Arguments:
- hidden: bfloat16 [24576, 2048], P('dp', 'vocab')
- gain: bfloat16 [2048], replicated, may hold values from 0.5 to 1.5
- head: bfloat16 [2048, 32000], P('dp', 'vocab')
- target_ids: int32 [24576], P('dp'), may hold values from 0 to 31999
- seq_lens: int32 [64], replicated, may hold values from 64 to 704, as said below
- seq_owner: int32 [64], replicated, may hold values from 0 to 31, as said below
Outputs:
- logprob: float32 [24576], P('dp')
- entropy: float32 [24576], P('dp')
Inputs may be any that keep to these rules, and one draw needn't show every extreme that they name: `seq_lens`: the lengths of the sequences owned by one dp index sum to at most 768; in every draw the sequences of some dp index sum to exactly 768. `seq_owner`: every dp index owns exactly 2 sequences.
All inputs are finite; a program needn't handle non-finite values.
Results may differ from a plain program's by a relative error of at most 0.0075.
Values may be sent and summed in bfloat16 or wider, within the bound.
A program may use at most 64 MiB of HBM per device.

v0:
```python
import jax
import jax.numpy as jnp
from jax import lax
from jax.sharding import PartitionSpec as P

EPS = 1e-05


def row_stats(normed, token_ids, columns, offset):
    count = normed.shape[0]
    width = normed.shape[1]
    block_rows = min(128, count)
    blocks = count // block_rows
    breadth = columns.shape[1]

    def compute(block_norm, block_ids):
        logits = jnp.dot(block_norm, columns, preferred_element_type=jnp.float32)
        top = jnp.max(logits, axis=1)
        expo = jnp.exp(logits - top[:, None])
        total = jnp.sum(expo, axis=1)
        weighted = jnp.sum(expo * logits, axis=1)
        local_id = block_ids - offset
        matches = jnp.arange(breadth, dtype=jnp.int32)[None, :] == local_id[:, None]
        picked = jnp.sum(jnp.where(matches, logits, 0.0), axis=1)
        return (top, total, weighted, picked)

    def per_block(item):
        block_norm, block_ids, start = item
        return compute(block_norm, block_ids)

    starts = jnp.arange(blocks, dtype=jnp.int32) * block_rows
    result = lax.map(
        per_block,
        (normed.reshape(blocks, block_rows, width), token_ids.reshape(blocks, block_rows), starts),
    )
    return tuple((member.reshape(count) for member in result))


def local(hidden, gain, head, target_ids, seq_lens, seq_owner):
    groups = lax.axis_size("dp")
    position = lax.axis_index("dp")
    slice_index = lax.axis_index("vocab")
    slots = hidden.shape[0]
    breadth = head.shape[1]
    owners = jnp.arange(groups, dtype=jnp.int32)
    loads = jnp.sum(jnp.where(seq_owner[:, None] == owners[None, :], seq_lens[:, None], 0), axis=0)
    own_live = jnp.arange(slots, dtype=jnp.int32) < loads[position]
    features = lax.all_gather(hidden, "vocab", axis=1, tiled=True)
    wide = features.astype(jnp.float32)
    normed = (
        wide
        * lax.rsqrt(jnp.mean(wide * wide, axis=1, keepdims=True) + EPS)
        * gain.astype(jnp.float32)
    ).astype(jnp.bfloat16)
    columns = lax.all_gather(head, "dp", axis=0, tiled=True)
    stats = row_stats(normed, target_ids, columns, slice_index * breadth)
    top = lax.pmax(stats[0], "vocab")
    factor = jnp.exp(stats[0] - top)
    total, weighted, picked = lax.psum((stats[1] * factor, stats[2] * factor, stats[3]), "vocab")
    lse = top + jnp.log(total)
    logprob = picked - lse
    entropy = lse - weighted / total
    return (jnp.where(own_live, logprob, 0.0), jnp.where(own_live, entropy, 0.0))


def solution(mesh):
    return jax.shard_map(
        local,
        mesh=mesh,
        in_specs=(P("dp", "vocab"), P(), P("dp", "vocab"), P("dp"), P(), P()),
        out_specs=(P("dp"), P("dp")),
        check_vma=False,
    )
```

profile of v0, /device:TPU:8, one launch (start us, length us, event | category | flops | bytes accessed | tf_op | source)
XLA Modules:
  0.0 306.3 jit_solution(14415921997200401669)
XLA Ops:
  7.2 0.0 all-gather.3.cloned.1.call-start
  7.2 0.7 all-gather.3.cloned.1.call-update
  7.9 0.0 all-gather.5.cloned.1.call-start
  7.9 0.7 all-gather.5.cloned.1.call-update
  8.7 0.7 convert_element_type.10
  9.4 0.8 select_reduce_fusion.1
  10.2 0.6 dynamic_slice.11
  10.8 36.1 %all-gather.3.cloned.1.call-done = bf16[768,2048]{1,0:T(8,128)(2,1)} async-done(((bf16[768,256]{1,0:T(8,128)(2,1)}), bf16[768,2048]{1,0:T(8,128)(2,1)}) %all-gather.3.cloned.1.call-update) | async-done | bytes 3145744 | tf_op jit(solution)/shard_map/all_gather | solution.py:48
  46.9 0.0 copy-start
  46.9 2.7 fusion.5
  49.6 0.1 copy-done
  49.7 2.5 fusion.7
  52.2 137.7 %all-gather.5.cloned.1.call-done = bf16[2048,4000]{1,0:T(8,128)(2,1)} async-done(((bf16[64,4000]{1,0:T(8,128)(2,1)}), bf16[2048,4000]{1,0:T(8,128)(2,1)}) %all-gather.5.cloned.1.call-update) | async-done | bytes 16384016 | tf_op jit(solution)/shard_map/all_gather | solution.py:55
  189.9 70.6 %while.16 = (s32[]{:T(128)}, f32[6,128]{1,0:T(8,128)S(1)}, f32[6,128]{1,0:T(8,128)S(1)}, f32[6,128]{1,0:T(8,128)S(1)}, f32[6,128]{1,0:T(8,128)S(1)}, /*index=5*/...) while((s32[]{:T(128)}, f32[6,128]{1,0:T(8,128)S(1)}, ...), condition=%wide.region_7.8_spmd, body=%wide.region_2.7_spmd.sunk | while | flops 2101247616 | bytes 21406340 | solution.py:32
  189.9 10.2 %fusion.13 = (f32[128]{0:T(128)S(1)}, f32[128,4000]{0,1:T(8,128)S(1)}) fusion(bf16[2048,4000]{1,0:T(8,128)(2,1)} %get-tuple-element.179, bf16[6,128,2048]{2,1,0:T(8,128)(2,1)} %get-tuple-element.178, s32[]{:T(128)} %get-tuple-element.162), kind=kOutput, calls=%fused_computation.25.clone.1 | convolution fusion | flops 2097663872 | bytes 19350528 | tf_op jit(solution)/shard_map/while/body/eval_jaxpr/dot_general | solution.py:17
  200.1 0.7 subtract_bitcast_fusion.2
  200.8 0.7 multiply_reduce_fusion.2
  201.6 10.2 %fusion.13 = (f32[128]{0:T(128)S(1)}, f32[128,4000]{0,1:T(8,128)S(1)}) fusion(bf16[2048,4000]{1,0:T(8,128)(2,1)} %get-tuple-element.179, bf16[6,128,2048]{2,1,0:T(8,128)(2,1)} %get-tuple-element.178, s32[]{:T(128)} %get-tuple-element.162), kind=kOutput, calls=%fused_computation.25.clone.1 | convolution fusion | flops 2097663872 | bytes 19350528 | tf_op jit(solution)/shard_map/while/body/eval_jaxpr/dot_general | solution.py:17
  211.9 0.7 subtract_bitcast_fusion.2
  212.6 0.7 multiply_reduce_fusion.2
  213.4 10.2 %fusion.13 = (f32[128]{0:T(128)S(1)}, f32[128,4000]{0,1:T(8,128)S(1)}) fusion(bf16[2048,4000]{1,0:T(8,128)(2,1)} %get-tuple-element.179, bf16[6,128,2048]{2,1,0:T(8,128)(2,1)} %get-tuple-element.178, s32[]{:T(128)} %get-tuple-element.162), kind=kOutput, calls=%fused_computation.25.clone.1 | convolution fusion | flops 2097663872 | bytes 19350528 | tf_op jit(solution)/shard_map/while/body/eval_jaxpr/dot_general | solution.py:17
  223.7 0.7 subtract_bitcast_fusion.2
  224.4 0.7 multiply_reduce_fusion.2
  225.2 10.2 %fusion.13 = (f32[128]{0:T(128)S(1)}, f32[128,4000]{0,1:T(8,128)S(1)}) fusion(bf16[2048,4000]{1,0:T(8,128)(2,1)} %get-tuple-element.179, bf16[6,128,2048]{2,1,0:T(8,128)(2,1)} %get-tuple-element.178, s32[]{:T(128)} %get-tuple-element.162), kind=kOutput, calls=%fused_computation.25.clone.1 | convolution fusion | flops 2097663872 | bytes 19350528 | tf_op jit(solution)/shard_map/while/body/eval_jaxpr/dot_general | solution.py:17
  235.4 0.7 subtract_bitcast_fusion.2
  236.1 0.7 multiply_reduce_fusion.2
  237.0 10.2 %fusion.13 = (f32[128]{0:T(128)S(1)}, f32[128,4000]{0,1:T(8,128)S(1)}) fusion(bf16[2048,4000]{1,0:T(8,128)(2,1)} %get-tuple-element.179, bf16[6,128,2048]{2,1,0:T(8,128)(2,1)} %get-tuple-element.178, s32[]{:T(128)} %get-tuple-element.162), kind=kOutput, calls=%fused_computation.25.clone.1 | convolution fusion | flops 2097663872 | bytes 19350528 | tf_op jit(solution)/shard_map/while/body/eval_jaxpr/dot_general | solution.py:17
  247.2 0.7 subtract_bitcast_fusion.2
  247.9 0.7 multiply_reduce_fusion.2
  248.7 10.2 %fusion.13 = (f32[128]{0:T(128)S(1)}, f32[128,4000]{0,1:T(8,128)S(1)}) fusion(bf16[2048,4000]{1,0:T(8,128)(2,1)} %get-tuple-element.179, bf16[6,128,2048]{2,1,0:T(8,128)(2,1)} %get-tuple-element.178, s32[]{:T(128)} %get-tuple-element.162), kind=kOutput, calls=%fused_computation.25.clone.1 | convolution fusion | flops 2097663872 | bytes 19350528 | tf_op jit(solution)/shard_map/while/body/eval_jaxpr/dot_general | solution.py:17
  259.0 0.7 subtract_bitcast_fusion.2
  259.7 0.7 multiply_reduce_fusion.2
  260.5 14.1 %pmax.7 = f32[768]{0:T(1024)S(1)} all-reduce(f32[768]{0:T(1024)S(1)} %bitcast.42), channel_id=1, replica_groups=mesh['dp'=32,'vocab'=8] {'vocab'}, use_global_device_ids=true, to_apply=%region_9.10 | all-reduce | flops 768 | bytes 6144 | tf_op jit(solution)/shard_map/pmax | solution.py:57
  274.7 23.6 %all-reduce = (f32[768]{0:T(1024)S(1)}, f32[768]{0:T(1024)S(1)}, f32[768]{0:T(1024)S(1)}) all-reduce(f32[768]{0:T(1024)S(1)} %bitcast.43, f32[768]{0:T(1024)S(1)} %get-tuple-element.85, f32[768]{0:T(1024)S(1)} %get-tuple-element.84), channel_id=1, replica_groups=mesh['dp'=32,'vocab'=8] {'vocab'}, use_global_device_ids=true, to_apply=%region_8.9 | all-reduce | flops 2304 | bytes 18432 | tf_op jit(solution)/shard_map/psum | solution.py:59
  298.2 1.2 subtract_select_fusion
  (30 shorter events, 0.8 us)
Async XLA Ops:
  7.2 39.7 %all-gather.3.cloned.1.call-start = ((), (), s32[]{:S(2)}) async-start(), calls=%async_computation | async-start | bytes 3538944 | tf_op jit(solution)/shard_map/all_gather | solution.py:48
  7.9 182.0 %all-gather.5.cloned.1.call-start = ((), (), s32[]{:S(2)}) async-start(), calls=%async_computation.1 | async-start | bytes 17301504 | tf_op jit(solution)/shard_map/all_gather | solution.py:55
  46.9 2.8 copy-start
Sparse Core Ops, SparseCore 0:
  9.8 37.0 all-gather.2
  49.5 140.3 all-gather.4
where the time goes:
time: 307 us; the launch traced here: 306 us
  waiting for transfers between devices  175 us (57%)
  matrix products  61.4 us (20%)
  blocking collectives  37.7 us (12%)
  other arithmetic  16.2 us (5%)
  between operations  14.1 us (5%)
    all_gather x1, waiting for transfers between devices, local(): columns = lax.all_gather(head, 'dp', axis=0, tiled=True)  138 us
    dot_general x6, matrix products, compute(): logits = jnp.dot(block_norm, columns, preferred_element_type=jnp.float32)  61.4 us
    all_gather x1, waiting for transfers between devices, local(): features = lax.all_gather(hidden, 'vocab', axis=1, tiled=True)  36.1 us
    psum x1, blocking collectives, local(): lax.psum((stats[1] * factor, stats[2] * factor, stats[3]), 'vocab')  23.6 us
    pmax x1, blocking collectives, local(): top = lax.pmax(stats[0], 'vocab')  14.1 us
  transfers between devices with their start and end apart: 2, of which 2 were waited for; matrix products, arithmetic and copies ran while one was open for 2% of the time, Pallas kernels for 0%

commit v1 on v0

--- a/solution.py
+++ b/solution.py
@@ -2,6 +2,7 @@
 import jax.numpy as jnp
 from jax import lax
 from jax.sharding import PartitionSpec as P
+from jax.lax import axis_index, axis_size, ppermute
 
 EPS = 1e-05
 
@@ -45,7 +46,18 @@
     owners = jnp.arange(groups, dtype=jnp.int32)
     loads = jnp.sum(jnp.where(seq_owner[:, None] == owners[None, :], seq_lens[:, None], 0), axis=0)
     own_live = jnp.arange(slots, dtype=jnp.int32) < loads[position]
-    features = lax.all_gather(hidden, "vocab", axis=1, tiled=True)
+
+    def name_spans_here(view, device_axis):
+        workers = axis_size(device_axis)
+        chunks = [view]
+        for b in range(workers - 1):
+            chunks.append(
+                ppermute(chunks[-1], device_axis, [(h, (h + 1) % workers) for h in range(workers)])
+            )
+        x_new = jnp.concatenate(chunks[::-1], axis=1)
+        return jnp.roll(x_new, shift=(axis_index(device_axis) + 1) * view.shape[1], axis=1)
+
+    features = name_spans_here(hidden, "vocab")
     wide = features.astype(jnp.float32)
     normed = (
         wide

time: 307 us -> 270 us (0.88)
  waiting for transfers between devices: 175 us -> 139 us
    ppermute x0 -> x7, waiting for transfers between devices: none -> 57 us  [name_spans_here(): ppermute(chunks[-1], device_axis, [(h, (h + 1) % workers) for h in range(...]
    all_gather x1, waiting for transfers between devices: 138 us -> 81.8 us  [local(): columns = lax.all_gather(head, 'dp', axis=0, tiled=True)]
    all_gather x1 -> x0, waiting for transfers between devices: 36.1 us -> none  [local(): features = lax.all_gather(hidden, 'vocab', axis=1, tiled=True)]
  transfers between devices with their start and end apart: 2 -> 8, of which waited for: 2 -> 8; matrix products, arithmetic and copies ran while one was open for 2% -> 2% of each run, Pallas kernels for 0% -> 0%
where the time goes in v1:
time: 270 us; the launch traced here: 269 us
  waiting for transfers between devices  139 us (51%)
  matrix products  61.4 us (23%)
  blocking collectives  37.7 us (14%)
  other arithmetic  14.2 us (5%)
  between operations  14.2 us (5%)
    all_gather x1, waiting for transfers between devices, local(): columns = lax.all_gather(head, 'dp', axis=0, tiled=True)  81.8 us
    dot_general x6, matrix products, compute(): logits = jnp.dot(block_norm, columns, preferred_element_type=jnp.float32)  61.4 us
    ppermute x7, waiting for transfers between devices, name_spans_here(): ppermute(chunks[-1], device_axis, [(h, (h + 1) % workers) for h in range(...  57 us
    psum x1, blocking collectives, local(): lax.psum((stats[1] * factor, stats[2] * factor, stats[3]), 'vocab')  23.6 us
    pmax x1, blocking collectives, local(): top = lax.pmax(stats[0], 'vocab')  14.1 us
  transfers between devices with their start and end apart: 8, of which 8 were waited for; matrix products, arithmetic and copies ran while one was open for 2% of the time, Pallas kernels for 0%

profile of v1, /device:TPU:8, one launch (start us, length us, event | category | flops | bytes accessed | tf_op | source)
XLA Modules:
  0.0 269.2 jit_solution(11210723892366828981)
XLA Ops:
  7.2 0.0 copy-start
  7.2 0.0 all-gather.2.cloned.1.call-start
  7.2 0.7 all-gather.2.cloned.1.call-update
  7.9 0.0 collective-permute-start
  7.9 8.6 %collective-permute-done = bf16[768,256]{1,0:T(8,128)(2,1)S(1)} collective-permute-done((bf16[768,256]{1,0:T(8,128)(2,1)}, bf16[768,256]{1,0:T(8,128)(2,1)S(1)}, u32[]{:S(2)}, u32[]{:S(2)}) %collective-permute-start) | collective-permute-done | bytes 393248 | tf_op jit(solution)/shard_map/ppermute | solution.py:55
  16.5 0.0 collective-permute-start.1
  16.5 8.4 %collective-permute-done.1 = bf16[768,256]{1,0:T(8,128)(2,1)S(1)} collective-permute-done((bf16[768,256]{1,0:T(8,128)(2,1)S(1)}, bf16[768,256]{1,0:T(8,128)(2,1)S(1)}, u32[]{:S(2)}, u32[]{:S(2)}) %collective-permute-start.1) | collective-permute-done | bytes 393248 | tf_op jit(solution)/shard_map/ppermute | solution.py:55
  25.0 0.0 collective-permute-start.2
  25.0 8.4 %collective-permute-done.2 = bf16[768,256]{1,0:T(8,128)(2,1)S(1)} collective-permute-done((bf16[768,256]{1,0:T(8,128)(2,1)S(1)}, bf16[768,256]{1,0:T(8,128)(2,1)S(1)}, u32[]{:S(2)}, u32[]{:S(2)}) %collective-permute-start.2) | collective-permute-done | bytes 393248 | tf_op jit(solution)/shard_map/ppermute | solution.py:55
  33.4 0.0 collective-permute-start.3
  33.4 8.4 %collective-permute-done.3 = bf16[768,256]{1,0:T(8,128)(2,1)S(1)} collective-permute-done((bf16[768,256]{1,0:T(8,128)(2,1)S(1)}, bf16[768,256]{1,0:T(8,128)(2,1)S(1)}, u32[]{:S(2)}, u32[]{:S(2)}) %collective-permute-start.3) | collective-permute-done | bytes 393248 | tf_op jit(solution)/shard_map/ppermute | solution.py:55
  41.8 0.0 collective-permute-start.4
  41.8 8.4 %collective-permute-done.4 = bf16[768,256]{1,0:T(8,128)(2,1)S(1)} collective-permute-done((bf16[768,256]{1,0:T(8,128)(2,1)S(1)}, bf16[768,256]{1,0:T(8,128)(2,1)S(1)}, u32[]{:S(2)}, u32[]{:S(2)}) %collective-permute-start.4) | collective-permute-done | bytes 393248 | tf_op jit(solution)/shard_map/ppermute | solution.py:55
  50.2 0.0 collective-permute-start.5
  50.2 8.4 %collective-permute-done.5 = bf16[768,256]{1,0:T(8,128)(2,1)S(1)} collective-permute-done((bf16[768,256]{1,0:T(8,128)(2,1)S(1)}, bf16[768,256]{1,0:T(8,128)(2,1)S(1)}, u32[]{:S(2)}, u32[]{:S(2)}) %collective-permute-start.5) | collective-permute-done | bytes 393248 | tf_op jit(solution)/shard_map/ppermute | solution.py:55
  58.6 0.0 collective-permute-start.6
  58.6 0.7 convert_element_type.10
  59.3 0.8 select_reduce_fusion.1
  60.1 0.6 dynamic_slice.15
  60.7 6.3 %collective-permute-done.6 = bf16[768,256]{1,0:T(8,128)(2,1)S(1)} collective-permute-done((bf16[768,256]{1,0:T(8,128)(2,1)S(1)}, bf16[768,256]{1,0:T(8,128)(2,1)S(1)}, u32[]{:S(2)}, u32[]{:S(2)}) %collective-permute-start.6) | collective-permute-done | bytes 393248 | tf_op jit(solution)/shard_map/ppermute | solution.py:55
  67.4 0.0 copy-done
  67.9 0.7 fusion.5
  68.6 2.5 fusion.7
  71.1 81.8 %all-gather.2.cloned.1.call-done = bf16[2048,4000]{1,0:T(8,128)(2,1)} async-done(((bf16[64,4000]{1,0:T(8,128)(2,1)}), bf16[2048,4000]{1,0:T(8,128)(2,1)}) %all-gather.2.cloned.1.call-update) | async-done | bytes 16384016 | tf_op jit(solution)/shard_map/all_gather | solution.py:67
  152.8 70.6 %while.16 = (s32[]{:T(128)}, f32[6,128]{1,0:T(8,128)S(1)}, f32[6,128]{1,0:T(8,128)S(1)}, f32[6,128]{1,0:T(8,128)S(1)}, f32[6,128]{1,0:T(8,128)S(1)}, /*index=5*/...) while((s32[]{:T(128)}, f32[6,128]{1,0:T(8,128)S(1)}, ...), condition=%wide.region_7.8_spmd, body=%wide.region_2.7_spmd.sunk | while | flops 2101247616 | bytes 21406340 | solution.py:33
  152.8 10.2 %fusion.13 = (f32[128]{0:T(128)S(1)}, f32[128,4000]{0,1:T(8,128)S(1)}) fusion(bf16[2048,4000]{1,0:T(8,128)(2,1)} %get-tuple-element.179, bf16[6,128,2048]{2,1,0:T(8,128)(2,1)} %get-tuple-element.178, s32[]{:T(128)} %get-tuple-element.162), kind=kOutput, calls=%fused_computation.41.clone.1 | convolution fusion | flops 2097663872 | bytes 19350528 | tf_op jit(solution)/shard_map/while/body/eval_jaxpr/dot_general | solution.py:18
  163.1 0.7 subtract_bitcast_fusion.2
  163.8 0.7 multiply_reduce_fusion.2
  164.6 10.2 %fusion.13 = (f32[128]{0:T(128)S(1)}, f32[128,4000]{0,1:T(8,128)S(1)}) fusion(bf16[2048,4000]{1,0:T(8,128)(2,1)} %get-tuple-element.179, bf16[6,128,2048]{2,1,0:T(8,128)(2,1)} %get-tuple-element.178, s32[]{:T(128)} %get-tuple-element.162), kind=kOutput, calls=%fused_computation.41.clone.1 | convolution fusion | flops 2097663872 | bytes 19350528 | tf_op jit(solution)/shard_map/while/body/eval_jaxpr/dot_general | solution.py:18
  174.8 0.7 subtract_bitcast_fusion.2
  175.5 0.7 multiply_reduce_fusion.2
  176.4 10.2 %fusion.13 = (f32[128]{0:T(128)S(1)}, f32[128,4000]{0,1:T(8,128)S(1)}) fusion(bf16[2048,4000]{1,0:T(8,128)(2,1)} %get-tuple-element.179, bf16[6,128,2048]{2,1,0:T(8,128)(2,1)} %get-tuple-element.178, s32[]{:T(128)} %get-tuple-element.162), kind=kOutput, calls=%fused_computation.41.clone.1 | convolution fusion | flops 2097663872 | bytes 19350528 | tf_op jit(solution)/shard_map/while/body/eval_jaxpr/dot_general | solution.py:18
  186.6 0.7 subtract_bitcast_fusion.2
  187.3 0.7 multiply_reduce_fusion.2
  188.1 10.2 %fusion.13 = (f32[128]{0:T(128)S(1)}, f32[128,4000]{0,1:T(8,128)S(1)}) fusion(bf16[2048,4000]{1,0:T(8,128)(2,1)} %get-tuple-element.179, bf16[6,128,2048]{2,1,0:T(8,128)(2,1)} %get-tuple-element.178, s32[]{:T(128)} %get-tuple-element.162), kind=kOutput, calls=%fused_computation.41.clone.1 | convolution fusion | flops 2097663872 | bytes 19350528 | tf_op jit(solution)/shard_map/while/body/eval_jaxpr/dot_general | solution.py:18
  198.4 0.7 subtract_bitcast_fusion.2
  199.1 0.7 multiply_reduce_fusion.2
  199.9 10.2 %fusion.13 = (f32[128]{0:T(128)S(1)}, f32[128,4000]{0,1:T(8,128)S(1)}) fusion(bf16[2048,4000]{1,0:T(8,128)(2,1)} %get-tuple-element.179, bf16[6,128,2048]{2,1,0:T(8,128)(2,1)} %get-tuple-element.178, s32[]{:T(128)} %get-tuple-element.162), kind=kOutput, calls=%fused_computation.41.clone.1 | convolution fusion | flops 2097663872 | bytes 19350528 | tf_op jit(solution)/shard_map/while/body/eval_jaxpr/dot_general | solution.py:18
  210.2 0.7 subtract_bitcast_fusion.2
  210.9 0.7 multiply_reduce_fusion.2
  211.7 10.2 %fusion.13 = (f32[128]{0:T(128)S(1)}, f32[128,4000]{0,1:T(8,128)S(1)}) fusion(bf16[2048,4000]{1,0:T(8,128)(2,1)} %get-tuple-element.179, bf16[6,128,2048]{2,1,0:T(8,128)(2,1)} %get-tuple-element.178, s32[]{:T(128)} %get-tuple-element.162), kind=kOutput, calls=%fused_computation.41.clone.1 | convolution fusion | flops 2097663872 | bytes 19350528 | tf_op jit(solution)/shard_map/while/body/eval_jaxpr/dot_general | solution.py:18
  221.9 0.7 subtract_bitcast_fusion.2
  222.6 0.7 multiply_reduce_fusion.2
  223.5 14.1 %pmax.7 = f32[768]{0:T(1024)S(1)} all-reduce(f32[768]{0:T(1024)S(1)} %bitcast.42), channel_id=1, replica_groups=mesh['dp'=32,'vocab'=8] {'vocab'}, use_global_device_ids=true, to_apply=%region_9.10 | all-reduce | flops 768 | bytes 6144 | tf_op jit(solution)/shard_map/pmax | solution.py:69
  237.6 23.6 %all-reduce = (f32[768]{0:T(1024)S(1)}, f32[768]{0:T(1024)S(1)}, f32[768]{0:T(1024)S(1)}) all-reduce(f32[768]{0:T(1024)S(1)} %bitcast.43, f32[768]{0:T(1024)S(1)} %get-tuple-element.85, f32[768]{0:T(1024)S(1)} %get-tuple-element.84), channel_id=1, replica_groups=mesh['dp'=32,'vocab'=8] {'vocab'}, use_global_device_ids=true, to_apply=%region_8.9 | all-reduce | flops 2304 | bytes 18432 | tf_op jit(solution)/shard_map/psum | solution.py:71
  261.2 1.2 subtract_select_fusion
  (46 shorter events, 1.6 us)
Async XLA Ops:
  7.2 60.2 %copy-start = (bf16[768,256]{1,0:T(8,128)(2,1)S(1)}, bf16[768,256]{1,0:T(8,128)(2,1)}, u32[]{:S(2)}) copy-start(bf16[768,256]{1,0:T(8,128)(2,1)} %param.8) | copy-start | bytes 1179652
  7.2 145.7 %all-gather.2.cloned.1.call-start = ((), (), s32[]{:S(2)}) async-start(), calls=%async_computation | async-start | bytes 17301504 | tf_op jit(solution)/shard_map/all_gather | solution.py:67
  7.9 8.6 %collective-permute-start = (bf16[768,256]{1,0:T(8,128)(2,1)}, bf16[768,256]{1,0:T(8,128)(2,1)S(1)}, u32[]{:S(2)}, u32[]{:S(2)}) collective-permute-start(bf16[768,256]{1,0:T(8,128)(2,1)} %param.8), channel_id=1, source_target_pairs={{0,1},{1,2},{2,3},{3,4},{4,5},{5,6},{6,7},{7,0},{8,9},{9,10},{10,1... | collective-permute-start | bytes 1179656 | tf_op jit(solution)/shard_map/ppermute | solution.py:55
  16.5 8.4 %collective-permute-start.1 = (bf16[768,256]{1,0:T(8,128)(2,1)S(1)}, bf16[768,256]{1,0:T(8,128)(2,1)S(1)}, u32[]{:S(2)}, u32[]{:S(2)}) collective-permute-start(bf16[768,256]{1,0:T(8,128)(2,1)S(1)} %collective-permute-done), channel_id=1, source_target_pairs={{0,1},{1,2},{2,3},{3,4},{4,5},{5,6},{6,7},{7,0},{8,9},{9,10},{10,1... | collective-permute-start | bytes 1179656 | tf_op jit(solution)/shard_map/ppermute | solution.py:55
  25.0 8.4 %collective-permute-start.2 = (bf16[768,256]{1,0:T(8,128)(2,1)S(1)}, bf16[768,256]{1,0:T(8,128)(2,1)S(1)}, u32[]{:S(2)}, u32[]{:S(2)}) collective-permute-start(bf16[768,256]{1,0:T(8,128)(2,1)S(1)} %collective-permute-done.1), channel_id=1, source_target_pairs={{0,1},{1,2},{2,3},{3,4},{4,5},{5,6},{6,7},{7,0},{8,9},{9,10},{10,1... | collective-permute-start | bytes 1179656 | tf_op jit(solution)/shard_map/ppermute | solution.py:55
  33.4 8.4 %collective-permute-start.3 = (bf16[768,256]{1,0:T(8,128)(2,1)S(1)}, bf16[768,256]{1,0:T(8,128)(2,1)S(1)}, u32[]{:S(2)}, u32[]{:S(2)}) collective-permute-start(bf16[768,256]{1,0:T(8,128)(2,1)S(1)} %collective-permute-done.2), channel_id=1, source_target_pairs={{0,1},{1,2},{2,3},{3,4},{4,5},{5,6},{6,7},{7,0},{8,9},{9,10},{10,1... | collective-permute-start | bytes 1179656 | tf_op jit(solution)/shard_map/ppermute | solution.py:55
  41.8 8.4 %collective-permute-start.4 = (bf16[768,256]{1,0:T(8,128)(2,1)S(1)}, bf16[768,256]{1,0:T(8,128)(2,1)S(1)}, u32[]{:S(2)}, u32[]{:S(2)}) collective-permute-start(bf16[768,256]{1,0:T(8,128)(2,1)S(1)} %collective-permute-done.3), channel_id=1, source_target_pairs={{0,1},{1,2},{2,3},{3,4},{4,5},{5,6},{6,7},{7,0},{8,9},{9,10},{10,1... | collective-permute-start | bytes 1179656 | tf_op jit(solution)/shard_map/ppermute | solution.py:55
  50.2 8.4 %collective-permute-start.5 = (bf16[768,256]{1,0:T(8,128)(2,1)S(1)}, bf16[768,256]{1,0:T(8,128)(2,1)S(1)}, u32[]{:S(2)}, u32[]{:S(2)}) collective-permute-start(bf16[768,256]{1,0:T(8,128)(2,1)S(1)} %collective-permute-done.4), channel_id=1, source_target_pairs={{0,1},{1,2},{2,3},{3,4},{4,5},{5,6},{6,7},{7,0},{8,9},{9,10},{10,1... | collective-permute-start | bytes 1179656 | tf_op jit(solution)/shard_map/ppermute | solution.py:55
  58.6 8.4 %collective-permute-start.6 = (bf16[768,256]{1,0:T(8,128)(2,1)S(1)}, bf16[768,256]{1,0:T(8,128)(2,1)S(1)}, u32[]{:S(2)}, u32[]{:S(2)}) collective-permute-start(bf16[768,256]{1,0:T(8,128)(2,1)S(1)} %collective-permute-done.5), channel_id=1, source_target_pairs={{0,1},{1,2},{2,3},{3,4},{4,5},{5,6},{6,7},{7,0},{8,9},{9,10},{10,1... | collective-permute-start | bytes 1179656 | tf_op jit(solution)/shard_map/ppermute | solution.py:55
Sparse Core Ops, SparseCore 0:
  10.6 142.1 all-gather.1
